TPU v7x, 128 devices: a whole 4x4x4 slice. The times are simulated.
128 devices in a mesh: ha: 16 (over z, y_lo, core), wa: 8 (over x, y_hi).
Axes of the slice: x: 4, y: 4 (y_hi: 2, y_lo: 2; y = y_hi * 2 + y_lo), z: 4, core: 2. Of those that a mesh axis runs over, the one named last changes fastest.
Arguments:
- tokens: bfloat16 [256, 256, 512], P('ha', 'wa'), may hold values from -40 to 40
- cotangent: bfloat16 [256, 256, 512], P('ha', 'wa'), may hold values from -6 to 6
- norm_gain: float32 [512], replicated, may hold values from 0.1 to 1.9
- in_weight: bfloat16 [512, 1536], replicated, may hold values from -0.25 to 0.25
- out_weight: bfloat16 [512, 512], replicated, may hold values from -0.25 to 0.25
- bias_table: float32 [16, 31, 31], replicated, may hold values from -256 to 256
Outputs:
- grad_input: bfloat16 [256, 256, 512], P('ha', 'wa')
- grad_table: float32 [16, 31, 31], replicated
All inputs are finite; a program needn't handle non-finite values.
Results may differ from a plain program's by a relative error of at most 0.011.
Values may be sent and summed in bfloat16 or wider, within the bound.
No kernel may reach another device: no remote copies, remote signals or barrier semaphores. Data moves between devices by JAX's collectives and lax.ppermute only.
A program may use at most 128 MiB of HBM per device.

v0:
```python
import jax
import jax.numpy as jnp
from jax import lax
from jax.sharding import PartitionSpec as P

D = 512
HEADS = 16
HEAD_DIM = 32
WIN = 16
TAB = 31
NORM_EPS = 1e-05


def offset_hot():
    places = jnp.arange(WIN)
    slot_ids = jnp.arange(TAB)
    return (
        places[:, None, None] - places[None, :, None] + (WIN - 1) == slot_ids[None, None, :]
    ).astype(jnp.float32)


def full_bias(bias_table, offset_table):
    partial_rows = jnp.einsum(
        "abd,hde->habe", offset_table, bias_table, precision=lax.Precision.HIGHEST
    )
    spread = jnp.einsum(
        "uve,habe->haubv", offset_table, partial_rows, precision=lax.Precision.HIGHEST
    )
    return spread.reshape(HEADS, WIN * WIN, WIN * WIN)


def group_grad(group_tokens, group_cot, norm_gain, in_weight, out_weight, bias_full, offset_table):
    group_rows = WIN * WIN
    tokens_wide = group_tokens.astype(jnp.float32)
    center = jnp.mean(tokens_wide, axis=-1, keepdims=True)
    shifted = tokens_wide - center
    inv_std = lax.rsqrt(jnp.mean(shifted * shifted, axis=-1, keepdims=True) + NORM_EPS)
    unit_rows = shifted * inv_std
    normed = (unit_rows * norm_gain).astype(jnp.bfloat16)
    mixed_rows = jnp.dot(normed, in_weight, preferred_element_type=jnp.float32)
    query_scale = HEAD_DIM ** (-0.5)
    queries = (
        (mixed_rows[:, :D] * query_scale).astype(jnp.bfloat16).reshape(group_rows, HEADS, HEAD_DIM)
    )
    key_rows = mixed_rows[:, D : 2 * D].astype(jnp.bfloat16).reshape(group_rows, HEADS, HEAD_DIM)
    values = mixed_rows[:, 2 * D :].astype(jnp.bfloat16).reshape(group_rows, HEADS, HEAD_DIM)
    scores = (
        jnp.einsum("thd,shd->hts", queries, key_rows, preferred_element_type=jnp.float32)
        + bias_full
    )
    row_top = jnp.max(scores, axis=-1, keepdims=True)
    exponent = jnp.exp(scores - row_top)
    attn_probs = exponent / jnp.sum(exponent, axis=-1, keepdims=True)
    probs_half = attn_probs.astype(jnp.bfloat16)
    grad_out = lax.dot_general(
        group_cot, out_weight, (((1,), (1,)), ((), ())), preferred_element_type=jnp.float32
    )
    grad_out = grad_out.astype(jnp.bfloat16).reshape(group_rows, HEADS, HEAD_DIM)
    grad_probs = jnp.einsum("thd,shd->hts", grad_out, values, preferred_element_type=jnp.float32)
    grad_values = jnp.einsum(
        "hts,thd->shd", probs_half, grad_out, preferred_element_type=jnp.float32
    ).astype(jnp.bfloat16)
    grad_scores = attn_probs * (
        grad_probs - jnp.sum(attn_probs * grad_probs, axis=-1, keepdims=True)
    )
    scores_half = grad_scores.astype(jnp.bfloat16)
    grad_queries = (
        jnp.einsum("hts,shd->thd", scores_half, key_rows, preferred_element_type=jnp.float32)
        * query_scale
    ).astype(jnp.bfloat16)
    grad_keys = jnp.einsum(
        "hts,thd->shd", scores_half, queries, preferred_element_type=jnp.float32
    ).astype(jnp.bfloat16)
    grad_mixed = jnp.concatenate(
        [
            grad_queries.reshape(group_rows, D),
            grad_keys.reshape(group_rows, D),
            grad_values.reshape(group_rows, D),
        ],
        axis=1,
    )
    grad_normed = lax.dot_general(
        grad_mixed, in_weight, (((1,), (1,)), ((), ())), preferred_element_type=jnp.float32
    )
    grad_unit = grad_normed * norm_gain
    grad_rows = inv_std * (
        grad_unit
        - jnp.mean(grad_unit, axis=-1, keepdims=True)
        - unit_rows * jnp.mean(grad_unit * unit_rows, axis=-1, keepdims=True)
    )
    folded = jnp.einsum(
        "haubv,uve->habe",
        grad_scores.reshape(HEADS, WIN, WIN, WIN, WIN),
        offset_table,
        precision=lax.Precision.HIGHEST,
    )
    table_part = jnp.einsum("habe,abd->hde", folded, offset_table, precision=lax.Precision.HIGHEST)
    return (grad_rows.astype(jnp.bfloat16), table_part)


def body(tokens, cotangent, norm_gain, in_weight, out_weight, bias_table):
    offset_table = offset_hot()
    bias_full = full_bias(bias_table, offset_table)
    high_parts = lax.axis_size("ha")
    wide_parts = lax.axis_size("wa")
    rows_local, cols_local, channels = tokens.shape
    row_steps = WIN // high_parts
    col_steps = WIN // wide_parts
    stride_h = rows_local // row_steps
    stride_w = cols_local // col_steps
    row_groups = stride_h // high_parts
    col_groups = stride_w // wide_parts
    group_count = row_groups * col_groups

    def to_layout(tile_block):
        laid = tile_block.reshape(
            row_steps, high_parts, row_groups, col_steps, wide_parts, col_groups, channels
        )
        laid = laid.transpose(2, 5, 1, 4, 0, 3, 6)
        return laid.reshape(group_count, high_parts, wide_parts, row_steps, col_steps, channels)

    def one_group(pair_rows):
        return group_grad(
            pair_rows[0], pair_rows[1], norm_gain, in_weight, out_weight, bias_full, offset_table
        )

    laid_tokens = to_layout(tokens)
    laid_cot = to_layout(cotangent)

    def swap_rows(laid):
        items = laid.shape[0]
        shaped = laid.reshape(items, high_parts, wide_parts, row_steps, col_steps, channels)
        return shaped.transpose(0, 1, 3, 2, 4, 5).reshape(items, WIN * WIN, channels)

    flat_shape = (group_count, high_parts * wide_parts, row_steps * col_steps, channels)
    grad_rows, table_parts = lax.map(
        one_group,
        (
            swap_rows(
                lax.all_to_all(
                    laid_tokens.reshape(flat_shape),
                    ("ha", "wa"),
                    split_axis=1,
                    concat_axis=1,
                    tiled=True,
                )
            ),
            swap_rows(
                lax.all_to_all(
                    laid_cot.reshape(flat_shape),
                    ("ha", "wa"),
                    split_axis=1,
                    concat_axis=1,
                    tiled=True,
                )
            ),
        ),
    )
    items = grad_rows.shape[0]
    shaped = grad_rows.reshape(items, high_parts, row_steps, wide_parts, col_steps, channels)
    grads_laid, table_parts = (
        shaped.transpose(0, 1, 3, 2, 4, 5).reshape(
            items, high_parts * wide_parts, row_steps * col_steps, channels
        ),
        table_parts,
    )
    returned = lax.all_to_all(grads_laid, ("ha", "wa"), split_axis=1, concat_axis=1, tiled=True)
    returned = returned.reshape(group_count, high_parts, wide_parts, row_steps, col_steps, channels)
    shaped = returned.reshape(
        row_groups, col_groups, high_parts, wide_parts, row_steps, col_steps, channels
    )
    shaped = shaped.transpose(4, 2, 0, 5, 3, 1, 6)
    grad_input = shaped.reshape(rows_local, cols_local, channels)
    grad_table = lax.psum(jnp.sum(table_parts, axis=0), ("ha", "wa"))
    return (grad_input, grad_table)


def solution(mesh):
    in_specs = (P("ha", "wa", None), P("ha", "wa", None), P(), P(), P(), P())
    out_specs = (P("ha", "wa", None), P())
    return jax.shard_map(body, mesh=mesh, in_specs=in_specs, out_specs=out_specs, check_vma=False)
```

profile of v0, /device:TPU:1, one launch (start us, length us, event | category | flops | bytes accessed | tf_op | source)
XLA Modules:
  0.0 330.3 jit_solution(11427729656623690947)
XLA Ops:
  0.6 1.3 reshape.82
  1.9 1.6 copy.72
  3.5 11.5 %all-to-all-start = ((bf16[2,128,2,512]{3,2,0,1:T(2,128)(2,1)}), bf16[2,128,2,512]{3,2,0,1:T(2,128)(2,1)S(1)}, u32[]{:S(2)}, u32[]{:S(2)}) async-start(bf16[2,128,2,512]{3,2,0,1:T(2,128)(2,1)} %bitcast.1), calls=%async_computation | async-start | bytes 1048576 | tf_op jit(solution)/shard_map/all_to_all | solution.py:140
  15.1 0.6 copy-done.11
  15.7 1.2 reshape.84
  17.0 1.6 copy.76
  18.6 1.0 fusion.54
  19.6 9.5 %all-to-all-done = bf16[2,128,2,512]{3,2,0,1:T(2,128)(2,1)S(1)} async-done(((bf16[2,128,2,512]{3,2,0,1:T(2,128)(2,1)}), bf16[2,128,2,512]{3,2,0,1:T(2,128)(2,1)S(1)}, u32[]{:S(2)}, u32[]{:S(2)}) %all-to-all-start) | async-done | bytes 524320 | tf_op jit(solution)/shard_map/all_to_all | solution.py:140
  29.1 4.7 %all-to-all-start.1 = ((bf16[2,128,2,512]{3,2,0,1:T(2,128)(2,1)}), bf16[2,128,2,512]{3,2,0,1:T(2,128)(2,1)}, u32[]{:S(2)}, u32[]{:S(2)}) async-start(bf16[2,128,2,512]{3,2,0,1:T(2,128)(2,1)} %bitcast.12), calls=%async_computation.1 | async-start | bytes 1048576 | tf_op jit(solution)/shard_map/all_to_all | solution.py:149
  33.8 17.4 %convolution_bitcast_fusion = f32[16,16,16,16,16]{4,3,2,1,0:T(8,128)} fusion(f32[16,16,16,31]{3,1,0,2:T(8,128)S(1)} %fusion.54, s32[16,16]{1,0:T(8,128)S(1)} %copy.74), kind=kOutput, calls=%fused_computation.64 | convolution fusion | flops 390078208 | bytes 4703232 | tf_op jit(solution)/shard_map/uve,habe->haubv/dot_general | solution.py:26
  51.2 23.5 %reshape.83 = f32[16,256,256]{2,1,0:T(8,128)} reshape(f32[16,16,16,16,16]{4,3,2,1,0:T(8,128)} %convolution_bitcast_fusion) | data formatting | bytes 8388608 | tf_op jit(solution)/shard_map/reshape | solution.py:29
  74.7 5.4 %copy.79 = f32[16,256,256]{1,2,0:T(8,128)} copy(f32[16,256,256]{2,1,0:T(8,128)} %reshape.83) | data formatting | bytes 8388608
  80.7 1.6 copy.77
  82.3 0.9 copy.80
  83.1 162.9 %while.14 = (s32[]{:T(128)}, bf16[2,256,512]{2,1,0:T(8,128)(2,1)}, f32[2,16,31,31]{2,3,1,0:T(8,128)}, bf16[2,256,512]{2,1,0:T(8,128)(2,1)S(1)}, f32[512]{0:T(512...) while((s32[]{:T(128)}, bf16[2,256,512]{2,1,0:T(8,128)(2,1)}, ...), condition=%wide.region_8.9_spmd.clone.clone, body=%wide.region_0.8_spmd.clone.clone.sunk | while | flops 1734164224 | bytes 137940368 | solution.py:136
  83.7 1.3 convolution_convert_fusion.4
  85.0 0.9 copy.105
  85.9 0.6 fusion.127
  86.5 0.8 fusion.128
  87.2 1.1 copy.106
  88.3 0.8 fusion.129
  89.2 1.1 copy.107
  90.3 1.1 copy.108
  91.3 2.9 convolution_add_fusion.2
  94.3 3.1 fusion.130
  97.5 5.2 %fusion.131 = bf16[16,32,256]{2,1,0:T(8,128)(2,1)} fusion(bf16[256,16,32]{0,2,1:T(8,128)(2,1)S(1)} %bitcast.193, f32[16,256]{1,0:T(8,128)S(1)} %get-tuple-element.273, f32[16,256,256]{1,2,0:T(8,128)} %copy-done.4), kind=kOutput, calls=%fused_computation.13.clone.1 | convolution fusion | flops 70390016 | bytes 4734976 | tf_op jit(solution)/shard_map/while/body/eval_jaxpr/hts,thd->shd/dot_general | solution.py:60
  102.7 3.2 multiply_reduce_fusion.2
  106.1 0.8 subtract_multiply_fusion.2
  106.9 0.5 fusion.132
  107.4 0.7 convolution_convert_fusion.5
  108.1 0.7 copy-done.2
  108.9 0.7 fusion.133
  109.6 0.9 fusion.134
  110.5 19.4 %reshape.111 = f32[16,16,16,16,16]{2,1,4,3,0:T(8,128)} reshape(f32[16,256,256]{1,2,0:T(8,128)} %copy-done.2) | data formatting | bytes 8388608 | tf_op jit(solution)/shard_map/while/body/eval_jaxpr/reshape | solution.py:93
  129.9 30.4 %fusion.135 = f32[16,16,16,31,1]{3,1,4,2,0:T(8,128)S(1)} fusion(f32[16,16,16,16,16]{2,1,4,3,0:T(8,128)} %reshape.111, s32[16,16]{0,1:T(8,128)S(1)} %get-tuple-element.314), kind=kOutput, calls=%fused_computation.53.clone.1 | convolution fusion | flops 390086144 | bytes 4703232 | tf_op jit(solution)/shard_map/while/body/eval_jaxpr/haubv,uve->habe/dot_general | solution.py:91
  160.4 3.5 %fusion.136 = f32[2,16,31,31]{2,3,1,0:T(8,128)S(1)} fusion(f32[2,16,31,31]{2,3,1,0:T(8,128)S(1)} %copy-done.13, s32[]{:T(128)S(6)} %copy.114, f32[16,16,16,31,1]{3,1,4,2,0:T(8,128)S(1)} %fusion.135, s32[16,16]{0,1:T(8,128)S(1)} %get-tuple-element.314), kind=kOutput, calls=%fused_computation.18.clone.1 | convolution fusion | flops 47250944 | bytes 2367492 | tf_op jit(solution)/shard_map/while/body/eval_jaxpr/habe,abd->hde/dot_general | solution.py:97
  163.9 0.8 copy-done.14
  165.0 1.3 convolution_convert_fusion.4
  166.3 0.9 copy.105
  167.2 0.6 fusion.127
  167.8 0.8 fusion.128
  168.6 1.1 copy.106
  169.7 0.8 fusion.129
  170.5 1.1 copy.107
  171.6 1.1 copy.108
  172.7 2.9 convolution_add_fusion.2
  175.6 3.1 fusion.130
  178.8 5.2 %fusion.131 = bf16[16,32,256]{2,1,0:T(8,128)(2,1)} fusion(bf16[256,16,32]{0,2,1:T(8,128)(2,1)S(1)} %bitcast.193, f32[16,256]{1,0:T(8,128)S(1)} %get-tuple-element.273, f32[16,256,256]{1,2,0:T(8,128)} %copy-done.4), kind=kOutput, calls=%fused_computation.13.clone.1 | convolution fusion | flops 70390016 | bytes 4734976 | tf_op jit(solution)/shard_map/while/body/eval_jaxpr/hts,thd->shd/dot_general | solution.py:60
  184.0 3.2 multiply_reduce_fusion.2
  187.5 0.8 subtract_multiply_fusion.2
  188.7 0.7 convolution_convert_fusion.5
  189.5 0.7 copy-done.2
  190.2 0.7 fusion.133
  190.9 0.9 fusion.134
  191.9 19.4 %reshape.111 = f32[16,16,16,16,16]{2,1,4,3,0:T(8,128)} reshape(f32[16,256,256]{1,2,0:T(8,128)} %copy-done.2) | data formatting | bytes 8388608 | tf_op jit(solution)/shard_map/while/body/eval_jaxpr/reshape | solution.py:93
  211.3 30.4 %fusion.135 = f32[16,16,16,31,1]{3,1,4,2,0:T(8,128)S(1)} fusion(f32[16,16,16,16,16]{2,1,4,3,0:T(8,128)} %reshape.111, s32[16,16]{0,1:T(8,128)S(1)} %get-tuple-element.314), kind=kOutput, calls=%fused_computation.53.clone.1 | convolution fusion | flops 390086144 | bytes 4703232 | tf_op jit(solution)/shard_map/while/body/eval_jaxpr/haubv,uve->habe/dot_general | solution.py:91
  241.7 3.5 %fusion.136 = f32[2,16,31,31]{2,3,1,0:T(8,128)S(1)} fusion(f32[2,16,31,31]{2,3,1,0:T(8,128)S(1)} %copy-done.13, s32[]{:T(128)S(6)} %copy.114, f32[16,16,16,31,1]{3,1,4,2,0:T(8,128)S(1)} %fusion.135, s32[16,16]{0,1:T(8,128)S(1)} %get-tuple-element.314), kind=kOutput, calls=%fused_computation.18.clone.1 | convolution fusion | flops 47250944 | bytes 2367492 | tf_op jit(solution)/shard_map/while/body/eval_jaxpr/habe,abd->hde/dot_general | solution.py:97
  245.2 0.8 copy-done.14
  246.0 2.4 copy.81
  248.4 9.9 %all-to-all-start.2 = ((bf16[2,128,2,512]{3,0,2,1:T(2,128)(2,1)}), bf16[2,128,2,512]{3,0,2,1:T(2,128)(2,1)S(1)}, u32[]{:S(2)}, u32[]{:S(2)}) async-start(bf16[2,128,2,512]{3,0,2,1:T(2,128)(2,1)} %bitcast.14), calls=%async_computation.2 | async-start | bytes 1048576 | tf_op jit(solution)/shard_map/all_to_all | solution.py:167
  258.3 1.1 reduce_sum.63
  259.4 68.6 %psum.7 = f32[16,31,31]{1,2,0:T(8,128)S(1)} all-reduce(f32[16,31,31]{1,2,0:T(8,128)S(1)} %reduce_sum.63), channel_id=1, replica_groups=mesh['ha'=16,'wa'=8] {'ha','wa'}, use_global_device_ids=true, to_apply=%region_10.11 | all-reduce | flops 15376 | bytes 123008 | tf_op jit(solution)/shard_map/psum | solution.py:174
  328.0 0.9 copy.85
  329.2 1.1 copy.84
  (66 shorter events, 2.8 us)
Async XLA Ops:
  0.6 18.0 %copy-start = (f32[16,31,31]{2,0,1:T(8,128)S(1)}, f32[16,31,31]{2,0,1:T(8,128)}, u32[]{:S(2)}) copy-start(f32[16,31,31]{2,0,1:T(8,128)} %param.13) | copy-start | bytes 184516
  3.5 25.5 %all-to-all-start = ((bf16[2,128,2,512]{3,2,0,1:T(2,128)(2,1)}), bf16[2,128,2,512]{3,2,0,1:T(2,128)(2,1)S(1)}, u32[]{:S(2)}, u32[]{:S(2)}) async-start(bf16[2,128,2,512]{3,2,0,1:T(2,128)(2,1)} %bitcast.1), calls=%async_computation | async-start | bytes 1048576 | tf_op jit(solution)/shard_map/all_to_all | solution.py:140
  15.0 0.6 copy-start.11
  29.1 22.1 %copy-start.9 = (bf16[2,128,2,512]{3,2,0,1:T(2,128)(2,1)}, bf16[2,128,2,512]{3,2,0,1:T(2,128)(2,1)S(1)}, u32[]{:S(2)}) copy-start(bf16[2,128,2,512]{3,2,0,1:T(2,128)(2,1)S(1)} %all-to-all-done) | copy-start | bytes 1572868
  29.1 51.6 %all-to-all-start.1 = ((bf16[2,128,2,512]{3,2,0,1:T(2,128)(2,1)}), bf16[2,128,2,512]{3,2,0,1:T(2,128)(2,1)}, u32[]{:S(2)}, u32[]{:S(2)}) async-start(bf16[2,128,2,512]{3,2,0,1:T(2,128)(2,1)} %bitcast.12), calls=%async_computation.1 | async-start | bytes 1048576 | tf_op jit(solution)/shard_map/all_to_all | solution.py:149
  74.7 5.4 %copy-start.10 = (bf16[2,128,2,512]{3,2,0,1:T(2,128)(2,1)S(1)}, bf16[2,128,2,512]{3,2,0,1:T(2,128)(2,1)}, u32[]{:S(2)}) copy-start(bf16[2,128,2,512]{3,2,0,1:T(2,128)(2,1)} %copy-done.9) | copy-start | bytes 1572868
  80.1 3.0 copy-start.5
  80.1 3.0 copy-start.6
  80.2 3.0 copy-start.12
  80.2 3.0 copy-start.15
  94.3 3.2 copy-start.4
  94.3 3.2 copy-start.8
  102.7 3.4 %copy-start.3 = (f32[16,256,256]{1,2,0:T(8,128)S(1)}, f32[16,256,256]{1,2,0:T(8,128)}, u32[]{:S(2)}) copy-start(f32[16,256,256]{1,2,0:T(8,128)} %get-tuple-element.274) | copy-start | bytes 12582916 | tf_op jit(solution)/shard_map/while
  106.9 2.0 copy-start.2
  106.9 2.0 copy-start.16
  129.9 30.4 %copy-start.13 = (f32[2,16,31,31]{2,3,1,0:T(8,128)S(1)}, f32[2,16,31,31]{2,3,1,0:T(8,128)}, u32[]{:S(2)}) copy-start(f32[2,16,31,31]{2,3,1,0:T(8,128)} %get-tuple-element.296) | copy-start | bytes 369028 | tf_op jit(solution)/shard_map/while
  129.9 34.7 %copy-start.7 = (bf16[512,512]{1,0:T(8,128)(2,1)S(1)}, bf16[512,512]{1,0:T(8,128)(2,1)}, u32[]{:S(2)}) copy-start(bf16[512,512]{1,0:T(8,128)(2,1)} %get-tuple-element.327) | copy-start | bytes 1572868 | tf_op jit(solution)/shard_map/while
  163.9 0.8 copy-start.14
  175.6 3.2 copy-start.4
  175.6 3.2 copy-start.8
  184.0 3.4 %copy-start.3 = (f32[16,256,256]{1,2,0:T(8,128)S(1)}, f32[16,256,256]{1,2,0:T(8,128)}, u32[]{:S(2)}) copy-start(f32[16,256,256]{1,2,0:T(8,128)} %get-tuple-element.274) | copy-start | bytes 12582916 | tf_op jit(solution)/shard_map/while
  188.2 2.0 copy-start.2
  188.2 2.0 copy-start.16
  211.3 30.4 %copy-start.13 = (f32[2,16,31,31]{2,3,1,0:T(8,128)S(1)}, f32[2,16,31,31]{2,3,1,0:T(8,128)}, u32[]{:S(2)}) copy-start(f32[2,16,31,31]{2,3,1,0:T(8,128)} %get-tuple-element.296) | copy-start | bytes 369028 | tf_op jit(solution)/shard_map/while
  211.3 34.7 %copy-start.7 = (bf16[512,512]{1,0:T(8,128)(2,1)S(1)}, bf16[512,512]{1,0:T(8,128)(2,1)}, u32[]{:S(2)}) copy-start(bf16[512,512]{1,0:T(8,128)(2,1)} %get-tuple-element.327) | copy-start | bytes 1572868 | tf_op jit(solution)/shard_map/while
  245.2 0.8 copy-start.14
  246.0 84.3 %copy-start.1 = (f32[16,31,31]{2,0,1:T(8,128)S(1)}, f32[16,31,31]{2,0,1:T(8,128)}, u32[]{:S(2)}) copy-start(f32[16,31,31]{2,0,1:T(8,128)} %param.13) | copy-start | bytes 184516
  248.4 80.5 %all-to-all-start.2 = ((bf16[2,128,2,512]{3,0,2,1:T(2,128)(2,1)}), bf16[2,128,2,512]{3,0,2,1:T(2,128)(2,1)S(1)}, u32[]{:S(2)}, u32[]{:S(2)}) async-start(bf16[2,128,2,512]{3,0,2,1:T(2,128)(2,1)} %bitcast.14), calls=%async_computation.2 | async-start | bytes 1048576 | tf_op jit(solution)/shard_map/all_to_all | solution.py:167
where the time goes:
time: 332 us; the launch traced here: 330 us
  matrix products  117 us (35%)
  local copies, waits for them, and re-layouts  95.5 us (29%)
  blocking collectives  68.6 us (21%)
  starting transfers between devices  26.1 us (8%)
  other arithmetic  12.9 us (4%)
  waiting for transfers between devices  9.46 us (3%)
    psum x1, blocking collectives, body(): grad_table = lax.psum(jnp.sum(table_parts, axis=0), ('ha', 'wa'))  68.6 us
    dot_general x2, matrix products, group_grad(): jnp.einsum('haubv,uve->habe', grad_scores.reshape(HEADS, WIN, WIN, WIN, W...  60.8 us
    reshape x2, local copies, waits for them, and re-layouts, group_grad(): grad_scores.reshape(HEADS, WIN, WIN, WIN, WIN)  38.8 us
    reshape x1, local copies, waits for them, and re-layouts, full_bias(): return spread.reshape(HEADS, WIN * WIN, WIN * WIN)  23.5 us
    dot_general x1, matrix products, full_bias(): jnp.einsum('uve,habe->haubv', offset_table, partial_rows, precision=lax.P...  17.4 us
    all_to_all x1, starting transfers between devices, body(): lax.all_to_all(laid_tokens.reshape(flat_shape), ('ha', 'wa'), split_axis=...  11.5 us
    dot_general x2, matrix products, group_grad(): jnp.einsum('hts,thd->shd', probs_half, grad_out, preferred_element_type=j...  10.3 us
    all_to_all x1, starting transfers between devices, body(): lax.all_to_all(grads_laid, ('ha', 'wa'), split_axis=1, concat_axis=1, til...  9.89 us
  transfers between devices with their start and end apart: 3, of which 1 were waited for; matrix products, arithmetic and copies ran while one was open for 16% of the time, Pallas kernels for 0%

commit v1 on v0

--- a/solution.py
+++ b/solution.py
@@ -2,6 +2,7 @@
 import jax.numpy as jnp
 from jax import lax
 from jax.sharding import PartitionSpec as P
+from jax.lax import psum
 
 D = 512
 HEADS = 16
@@ -171,7 +172,9 @@
     )
     shaped = shaped.transpose(4, 2, 0, 5, 3, 1, 6)
     grad_input = shaped.reshape(rows_local, cols_local, channels)
-    grad_table = lax.psum(jnp.sum(table_parts, axis=0), ("ha", "wa"))
+    message = jnp.sum(table_parts, axis=0)
+    new = psum(message, axis_name="ha")
+    grad_table = psum(new, "wa")
     return (grad_input, grad_table)
 
 

time: 332 us -> 367 us (1.11)
  the two profiles are of different devices: /device:TPU:1 before, /device:TPU:0 now
where the time goes in v1:
time: 367 us; the launch traced here: 365 us
  matrix products  116 us (32%)
  blocking collectives  103 us (28%)
  local copies, waits for them, and re-layouts  95.4 us (26%)
  starting transfers between devices  26.6 us (7%)
  other arithmetic  12.9 us (4%)
  waiting for transfers between devices  8.62 us (2%)
    dot_general x2, matrix products, group_grad(): jnp.einsum('haubv,uve->habe', grad_scores.reshape(HEADS, WIN, WIN, WIN, W...  60.8 us
    psum x1, blocking collectives, body(): new = psum(message, axis_name='ha')  59 us
    psum x1, blocking collectives, body(): grad_table = psum(new, 'wa')  44.4 us
    reshape x2, local copies, waits for them, and re-layouts, group_grad(): grad_scores.reshape(HEADS, WIN, WIN, WIN, WIN)  38.8 us
    reshape x1, local copies, waits for them, and re-layouts, full_bias(): return spread.reshape(HEADS, WIN * WIN, WIN * WIN)  23.5 us
    dot_general x1, matrix products, full_bias(): jnp.einsum('uve,habe->haubv', offset_table, partial_rows, precision=lax.P...  17.4 us
    all_to_all x1, starting transfers between devices, body(): lax.all_to_all(laid_tokens.reshape(flat_shape), ('ha', 'wa'), split_axis=...  11.2 us
    dot_general x2, matrix products, group_grad(): jnp.einsum('hts,thd->shd', probs_half, grad_out, preferred_element_type=j...  10.3 us
  transfers between devices with their start and end apart: 3, of which 1 were waited for; matrix products, arithmetic and copies ran while one was open for 14% of the time, Pallas kernels for 0%

profile of v1, /device:TPU:0, one launch (start us, length us, event | category | flops | bytes accessed | tf_op | source)
XLA Modules:
  0.0 364.7 jit_solution(2962486937305774323)
XLA Ops:
  0.6 1.3 reshape.82
  1.9 1.6 copy.72
  3.5 11.2 %all-to-all-start = ((bf16[2,128,2,512]{3,2,0,1:T(2,128)(2,1)}), bf16[2,128,2,512]{3,2,0,1:T(2,128)(2,1)S(1)}, u32[]{:S(2)}, u32[]{:S(2)}) async-start(bf16[2,128,2,512]{3,2,0,1:T(2,128)(2,1)} %bitcast.1), calls=%async_computation | async-start | bytes 1048576 | tf_op jit(solution)/shard_map/all_to_all | solution.py:141
  14.7 0.6 copy-done.11
  15.4 1.2 reshape.84
  16.6 1.6 copy.76
  18.3 1.0 fusion.54
  19.3 8.6 %all-to-all-done = bf16[2,128,2,512]{3,2,0,1:T(2,128)(2,1)S(1)} async-done(((bf16[2,128,2,512]{3,2,0,1:T(2,128)(2,1)}), bf16[2,128,2,512]{3,2,0,1:T(2,128)(2,1)S(1)}, u32[]{:S(2)}, u32[]{:S(2)}) %all-to-all-start) | async-done | bytes 524320 | tf_op jit(solution)/shard_map/all_to_all | solution.py:141
  27.9 5.7 %all-to-all-start.1 = ((bf16[2,128,2,512]{3,2,0,1:T(2,128)(2,1)}), bf16[2,128,2,512]{3,2,0,1:T(2,128)(2,1)}, u32[]{:S(2)}, u32[]{:S(2)}) async-start(bf16[2,128,2,512]{3,2,0,1:T(2,128)(2,1)} %bitcast.12), calls=%async_computation.1 | async-start | bytes 1048576 | tf_op jit(solution)/shard_map/all_to_all | solution.py:150
  33.7 17.4 %convolution_bitcast_fusion = f32[16,16,16,16,16]{4,3,2,1,0:T(8,128)} fusion(f32[16,16,16,31]{3,1,0,2:T(8,128)S(1)} %fusion.54, s32[16,16]{1,0:T(8,128)S(1)} %copy.74), kind=kOutput, calls=%fused_computation.64 | convolution fusion | flops 390078208 | bytes 4703232 | tf_op jit(solution)/shard_map/uve,habe->haubv/dot_general | solution.py:27
  51.1 23.5 %reshape.83 = f32[16,256,256]{2,1,0:T(8,128)} reshape(f32[16,16,16,16,16]{4,3,2,1,0:T(8,128)} %convolution_bitcast_fusion) | data formatting | bytes 8388608 | tf_op jit(solution)/shard_map/reshape | solution.py:30
  74.6 5.4 %copy.79 = f32[16,256,256]{1,2,0:T(8,128)} copy(f32[16,256,256]{2,1,0:T(8,128)} %reshape.83) | data formatting | bytes 8388608
  80.6 1.6 copy.77
  82.2 0.9 copy.80
  83.0 162.7 %while.14 = (s32[]{:T(128)}, bf16[2,256,512]{2,1,0:T(8,128)(2,1)}, f32[2,16,31,31]{2,3,1,0:T(8,128)}, bf16[2,256,512]{2,1,0:T(8,128)(2,1)S(1)}, f32[512]{0:T(512...) while((s32[]{:T(128)}, bf16[2,256,512]{2,1,0:T(8,128)(2,1)}, ...), condition=%wide.region_8.9_spmd.clone.clone, body=%wide.region_0.8_spmd.clone.clone.sunk | while | flops 1734164224 | bytes 137940368 | solution.py:137
  83.6 1.3 convolution_convert_fusion.4
  84.9 0.8 copy.105
  85.7 0.6 fusion.127
  86.4 0.7 fusion.128
  87.1 1.1 copy.106
  88.2 0.8 fusion.129
  89.0 1.1 copy.107
  90.1 1.1 copy.108
  91.2 2.9 convolution_add_fusion.2
  94.2 3.1 fusion.130
  97.3 5.1 %fusion.131 = bf16[16,32,256]{2,1,0:T(8,128)(2,1)} fusion(bf16[256,16,32]{0,2,1:T(8,128)(2,1)S(1)} %bitcast.193, f32[16,256]{1,0:T(8,128)S(1)} %get-tuple-element.273, f32[16,256,256]{1,2,0:T(8,128)} %copy-done.4), kind=kOutput, calls=%fused_computation.13.clone.1 | convolution fusion | flops 70390016 | bytes 4734976 | tf_op jit(solution)/shard_map/while/body/eval_jaxpr/hts,thd->shd/dot_general | solution.py:61
  102.5 3.2 multiply_reduce_fusion.2
  105.9 0.8 subtract_multiply_fusion.2
  107.2 0.7 convolution_convert_fusion.5
  107.9 0.7 copy-done.2
  108.7 0.7 fusion.133
  109.4 0.9 fusion.134
  110.3 19.4 %reshape.111 = f32[16,16,16,16,16]{2,1,4,3,0:T(8,128)} reshape(f32[16,256,256]{1,2,0:T(8,128)} %copy-done.2) | data formatting | bytes 8388608 | tf_op jit(solution)/shard_map/while/body/eval_jaxpr/reshape | solution.py:94
  129.8 30.4 %fusion.135 = f32[16,16,16,31,1]{3,1,4,2,0:T(8,128)S(1)} fusion(f32[16,16,16,16,16]{2,1,4,3,0:T(8,128)} %reshape.111, s32[16,16]{0,1:T(8,128)S(1)} %get-tuple-element.314), kind=kOutput, calls=%fused_computation.53.clone.1 | convolution fusion | flops 390086144 | bytes 4703232 | tf_op jit(solution)/shard_map/while/body/eval_jaxpr/haubv,uve->habe/dot_general | solution.py:92
  160.2 3.5 fusion.136
  163.7 0.8 copy-done.14
  164.9 1.3 convolution_convert_fusion.4
  166.2 0.8 copy.105
  167.0 0.6 fusion.127
  167.6 0.7 fusion.128
  168.4 1.1 copy.106
  169.5 0.8 fusion.129
  170.3 1.1 copy.107
  171.4 1.1 copy.108
  172.5 2.9 convolution_add_fusion.2
  175.4 3.1 fusion.130
  178.6 5.1 %fusion.131 = bf16[16,32,256]{2,1,0:T(8,128)(2,1)} fusion(bf16[256,16,32]{0,2,1:T(8,128)(2,1)S(1)} %bitcast.193, f32[16,256]{1,0:T(8,128)S(1)} %get-tuple-element.273, f32[16,256,256]{1,2,0:T(8,128)} %copy-done.4), kind=kOutput, calls=%fused_computation.13.clone.1 | convolution fusion | flops 70390016 | bytes 4734976 | tf_op jit(solution)/shard_map/while/body/eval_jaxpr/hts,thd->shd/dot_general | solution.py:61
  183.8 3.2 multiply_reduce_fusion.2
  187.2 0.8 subtract_multiply_fusion.2
  188.5 0.7 convolution_convert_fusion.5
  189.2 0.7 copy-done.2
  189.9 0.7 fusion.133
  190.7 0.9 fusion.134
  191.6 19.4 %reshape.111 = f32[16,16,16,16,16]{2,1,4,3,0:T(8,128)} reshape(f32[16,256,256]{1,2,0:T(8,128)} %copy-done.2) | data formatting | bytes 8388608 | tf_op jit(solution)/shard_map/while/body/eval_jaxpr/reshape | solution.py:94
  211.0 30.4 %fusion.135 = f32[16,16,16,31,1]{3,1,4,2,0:T(8,128)S(1)} fusion(f32[16,16,16,16,16]{2,1,4,3,0:T(8,128)} %reshape.111, s32[16,16]{0,1:T(8,128)S(1)} %get-tuple-element.314), kind=kOutput, calls=%fused_computation.53.clone.1 | convolution fusion | flops 390086144 | bytes 4703232 | tf_op jit(solution)/shard_map/while/body/eval_jaxpr/haubv,uve->habe/dot_general | solution.py:92
  241.4 3.5 fusion.136
  245.0 0.8 copy-done.14
  245.8 2.4 copy.81
  248.2 9.7 %all-to-all-start.2 = ((bf16[2,128,2,512]{3,0,2,1:T(2,128)(2,1)}), bf16[2,128,2,512]{3,0,2,1:T(2,128)(2,1)S(1)}, u32[]{:S(2)}, u32[]{:S(2)}) async-start(bf16[2,128,2,512]{3,0,2,1:T(2,128)(2,1)} %bitcast.14), calls=%async_computation.2 | async-start | bytes 1048576 | tf_op jit(solution)/shard_map/all_to_all | solution.py:168
  257.9 1.1 reduce_sum.63
  259.0 59.0 %psum.14 = f32[16,31,31]{1,2,0:T(8,128)S(1)} all-reduce(f32[16,31,31]{1,2,0:T(8,128)S(1)} %reduce_sum.63), channel_id=1, replica_groups=mesh['ha'=16,'wa'=8] {'ha'}, use_global_device_ids=true, to_apply=%region_10.11 | all-reduce | flops 15376 | bytes 123008 | tf_op jit(solution)/shard_map/psum | solution.py:176
  318.0 44.4 %psum.15 = f32[16,31,31]{1,2,0:T(8,128)S(1)} all-reduce(f32[16,31,31]{1,2,0:T(8,128)S(1)} %psum.14), channel_id=1, replica_groups=mesh['ha'=16,'wa'=8] {'wa'}, use_global_device_ids=true, to_apply=%region_11.12 | all-reduce | flops 15376 | bytes 123008 | tf_op jit(solution)/shard_map/psum | solution.py:177
  362.4 0.9 copy.85
  363.6 1.1 copy.84
  (67 shorter events, 3.3 us)
Async XLA Ops:
  0.6 17.6 %copy-start = (f32[16,31,31]{2,0,1:T(8,128)S(1)}, f32[16,31,31]{2,0,1:T(8,128)}, u32[]{:S(2)}) copy-start(f32[16,31,31]{2,0,1:T(8,128)} %param.13) | copy-start | bytes 184516
  3.5 24.4 %all-to-all-start = ((bf16[2,128,2,512]{3,2,0,1:T(2,128)(2,1)}), bf16[2,128,2,512]{3,2,0,1:T(2,128)(2,1)S(1)}, u32[]{:S(2)}, u32[]{:S(2)}) async-start(bf16[2,128,2,512]{3,2,0,1:T(2,128)(2,1)} %bitcast.1), calls=%async_computation | async-start | bytes 1048576 | tf_op jit(solution)/shard_map/all_to_all | solution.py:141
  14.7 0.6 copy-start.11
  27.9 23.2 %copy-start.9 = (bf16[2,128,2,512]{3,2,0,1:T(2,128)(2,1)}, bf16[2,128,2,512]{3,2,0,1:T(2,128)(2,1)S(1)}, u32[]{:S(2)}) copy-start(bf16[2,128,2,512]{3,2,0,1:T(2,128)(2,1)S(1)} %all-to-all-done) | copy-start | bytes 1572868
  27.9 52.6 %all-to-all-start.1 = ((bf16[2,128,2,512]{3,2,0,1:T(2,128)(2,1)}), bf16[2,128,2,512]{3,2,0,1:T(2,128)(2,1)}, u32[]{:S(2)}, u32[]{:S(2)}) async-start(bf16[2,128,2,512]{3,2,0,1:T(2,128)(2,1)} %bitcast.12), calls=%async_computation.1 | async-start | bytes 1048576 | tf_op jit(solution)/shard_map/all_to_all | solution.py:150
  74.6 5.4 %copy-start.10 = (bf16[2,128,2,512]{3,2,0,1:T(2,128)(2,1)S(1)}, bf16[2,128,2,512]{3,2,0,1:T(2,128)(2,1)}, u32[]{:S(2)}) copy-start(bf16[2,128,2,512]{3,2,0,1:T(2,128)(2,1)} %copy-done.9) | copy-start | bytes 1572868
  80.0 3.0 copy-start.5
  80.0 3.0 copy-start.6
  80.0 3.0 copy-start.12
  80.1 3.0 copy-start.15
  94.2 3.2 copy-start.4
  94.2 3.2 copy-start.8
  102.5 3.4 copy-start.3
  106.7 1.9 copy-start.2
  106.7 1.9 copy-start.16
  129.8 30.4 %copy-start.13 = (f32[2,16,31,31]{2,3,1,0:T(8,128)S(1)}, f32[2,16,31,31]{2,3,1,0:T(8,128)}, u32[]{:S(2)}) copy-start(f32[2,16,31,31]{2,3,1,0:T(8,128)} %get-tuple-element.296) | copy-start | bytes 369028 | tf_op jit(solution)/shard_map/while
  129.8 34.7 %copy-start.7 = (bf16[512,512]{1,0:T(8,128)(2,1)S(1)}, bf16[512,512]{1,0:T(8,128)(2,1)}, u32[]{:S(2)}) copy-start(bf16[512,512]{1,0:T(8,128)(2,1)} %get-tuple-element.327) | copy-start | bytes 1572868 | tf_op jit(solution)/shard_map/while
  163.7 0.8 copy-start.14
  175.4 3.2 copy-start.4
  175.4 3.2 copy-start.8
  183.8 3.4 copy-start.3
  188.0 1.9 copy-start.2
  188.0 1.9 copy-start.16
  211.0 30.4 %copy-start.13 = (f32[2,16,31,31]{2,3,1,0:T(8,128)S(1)}, f32[2,16,31,31]{2,3,1,0:T(8,128)}, u32[]{:S(2)}) copy-start(f32[2,16,31,31]{2,3,1,0:T(8,128)} %get-tuple-element.296) | copy-start | bytes 369028 | tf_op jit(solution)/shard_map/while
  211.0 34.7 %copy-start.7 = (bf16[512,512]{1,0:T(8,128)(2,1)S(1)}, bf16[512,512]{1,0:T(8,128)(2,1)}, u32[]{:S(2)}) copy-start(bf16[512,512]{1,0:T(8,128)(2,1)} %get-tuple-element.327) | copy-start | bytes 1572868 | tf_op jit(solution)/shard_map/while
  244.9 0.8 copy-start.14
  245.8 118.9 %copy-start.1 = (f32[16,31,31]{2,0,1:T(8,128)S(1)}, f32[16,31,31]{2,0,1:T(8,128)}, u32[]{:S(2)}) copy-start(f32[16,31,31]{2,0,1:T(8,128)} %param.13) | copy-start | bytes 184516
  248.2 115.2 %all-to-all-start.2 = ((bf16[2,128,2,512]{3,0,2,1:T(2,128)(2,1)}), bf16[2,128,2,512]{3,0,2,1:T(2,128)(2,1)S(1)}, u32[]{:S(2)}, u32[]{:S(2)}) async-start(bf16[2,128,2,512]{3,0,2,1:T(2,128)(2,1)} %bitcast.14), calls=%async_computation.2 | async-start | bytes 1048576 | tf_op jit(solution)/shard_map/all_to_all | solution.py:168
